TPU v7x, 128 devices: a whole 4x4x4 slice. The times are simulated.
128 devices in a mesh: row: 4 (over z_hi, core), col: 32 (over z_lo, x, y).
Axes of the slice: x: 4, y: 4, z: 4 (z_hi: 2, z_lo: 2; z = z_hi * 2 + z_lo), core: 2. Of those that a mesh axis runs over, the one named last changes fastest.
Arguments:
- derivs: bfloat16 [1024, 65536], P(('row', 'col')), may hold values from -15 to 15, as said below
- energy_derivs: bfloat16 [1024, 65536], P(('row', 'col')), may hold values from -15 to 15, as said below
- energies: float32 [1024], P(('row', 'col')), may hold values from -30 to -10, as said below
Outputs:
- correlation: float32 [4096, 65536], P('row', 'col')
- hamiltonian: float32 [4096, 65536], P('row', 'col')
Inputs may be any that keep to these rules, and one draw needn't show every extreme that they name: `derivs`: finite values. `energy_derivs`: finite values. `energies`: finite values.
All inputs are finite; a program needn't handle non-finite values.
Results may differ from a plain program's by a relative error of at most 0.0041.
Values may be sent and summed in bfloat16 or wider, within the bound.
A program may use at most 128 MiB of HBM per device.

v0:
```python
import jax
import jax.numpy as jnp
from jax import lax
from jax.sharding import PartitionSpec as P


def in_order(parts, dim):
    shape = list(parts.shape[1:])
    shape[dim] *= parts.shape[0]
    return jnp.moveaxis(parts, 0, dim).reshape(shape)


def from_everyone(shard, axis):
    count = lax.axis_size(axis)
    return lax.all_to_all(
        jnp.broadcast_to(shard[None], (count, *shard.shape)), axis, 0, 0, tiled=True
    )


def gathered_copies(shard, axis, dim):
    return in_order(from_everyone(shard, axis), dim)


def taken_together(shard, axis):
    return from_everyone(shard, axis).sum(axis=0)


def in_one(arrays, axis):
    ends = [0]
    for a in arrays:
        ends.append(ends[-1] + a.size)
    running = taken_together(jnp.concatenate([a.ravel() for a in arrays]), axis)
    return tuple((running[b:e].reshape(a.shape) for a, b, e in zip(arrays, ends, ends[1:])))


def in_one_piece(arrays, axis, dim, along):
    ends, at = ([], 0)
    for a in arrays[:-1]:
        at += a.shape[along]
        ends.append(at)
    both = jnp.concatenate(arrays, axis=along)
    return tuple(jnp.split(lax.all_gather(both, axis, axis=dim, tiled=True), ends, axis=along))


def contract(row_block, other):
    return lax.dot_general(
        row_block, other, (((0,), (0,)), ((), ())), preferred_element_type=jnp.float32
    )


def centre_tiles(raw_derivs, raw_grads, sample_energy, mean_derivs, mean_grads, mean_energy):
    offsets = raw_derivs.astype(jnp.float32) - mean_derivs[None, :]
    centred = offsets.astype(jnp.bfloat16)
    shifted = (sample_energy - mean_energy)[:, None] * offsets
    energy_term = (shifted + (raw_grads.astype(jnp.float32) - mean_grads[None, :])).astype(
        jnp.bfloat16
    )
    return (centred, energy_term)


def to_row_major(matrix, row_count, col_count):
    return (
        matrix.reshape((col_count, row_count, -1) + matrix.shape[1:])
        .swapaxes(0, 1)
        .reshape(matrix.shape)
    )


def fetch_rows(source):
    portion = lax.all_to_all(source, "row", split_axis=1, concat_axis=0, tiled=True)
    return (gathered_copies(portion, "col", 0), "col_major")


def body(derivs, energy_derivs, energies):
    row_count = lax.axis_size("row")
    col_count = lax.axis_size("col")
    local_count = derivs.shape[0]
    total_count = local_count * row_count * col_count
    slab_width = derivs.shape[1] // 16
    every_energy = lax.all_gather(energies, ("row", "col"), axis=0, tiled=True)
    mean_energy = jnp.sum(every_energy) / total_count
    moving = (derivs, energy_derivs)
    row_source = derivs[:, :slab_width]
    row_data, row_order = fetch_rows(row_source)
    row_full = row_data.astype(jnp.float32)
    row_data = (row_full - (jnp.sum(row_full, axis=0) / total_count)[None, :]).astype(jnp.bfloat16)
    tiles = (
        lax.all_to_all(moving[0], "col", split_axis=1, concat_axis=0, tiled=True),
        lax.all_to_all(moving[1], "col", split_axis=1, concat_axis=0, tiled=True),
    )
    tile_totals = in_one(
        (
            jnp.sum(tiles[0].astype(jnp.float32), axis=0),
            jnp.sum(tiles[1].astype(jnp.float32), axis=0),
        ),
        "row",
    )
    group_energy = lax.dynamic_slice_in_dim(
        every_energy, lax.axis_index("row") * (col_count * local_count), col_count * local_count, 0
    )
    tiles = centre_tiles(
        tiles[0],
        tiles[1],
        group_energy,
        tile_totals[0] / total_count,
        tile_totals[1] / total_count,
        mean_energy,
    )
    row_data = to_row_major(row_data, row_count, col_count)
    pieces = in_one_piece((tiles[0], tiles[1]), "row", 0, 1)
    correlation_sum = contract(row_data, pieces[0])
    hamil_sum = contract(row_data, pieces[1])
    return (correlation_sum / total_count, hamil_sum / total_count)


def solution(mesh):
    placed = (P(("row", "col"), None), P(("row", "col"), None), P(("row", "col")))
    return jax.shard_map(
        body,
        mesh=mesh,
        in_specs=placed,
        out_specs=(P("row", "col"), P("row", "col")),
        check_vma=False,
    )
```

profile of v0, /device:TPU:1, one launch (start us, length us, event | category | flops | bytes accessed | tf_op | source)
XLA Modules:
  0.0 226.9 jit_solution(6114730589227121759)
XLA Ops:
  7.2 0.0 copy-start.1
  7.2 24.4 %all_to_all.53 = bf16[8,32,2048]{2,0,1:T(8,128)(2,1)S(1)} all-to-all(bf16[8,32,2048]{2,0,1:T(8,128)(2,1)} %bitcast.43), channel_id=1, replica_groups=mesh['row'=4,'col'=32] {'col'}, dimensions={1} | all-to-all | bytes 2097152 | tf_op jit(solution)/shard_map/all_to_all | solution.py:89
  31.6 4.9 %all-to-all-start.2 = ((bf16[8,32,2048]{2,0,1:T(8,128)(2,1)}), bf16[8,32,2048]{2,0,1:T(8,128)(2,1)S(1)}, u32[]{:S(2)}, u32[]{:S(2)}) async-start(bf16[8,32,2048]{2,0,1:T(8,128)(2,1)} %bitcast.6), calls=%async_computation.2 | async-start | bytes 2097152 | tf_op jit(solution)/shard_map/all_to_all | solution.py:88
  36.6 0.0 copy-done.1
  36.6 0.2 dynamic-update-slice
  36.8 71.1 %all-reduce = f32[1024]{0:T(1024)S(1)} all-reduce(f32[1024]{0:T(1024)S(1)} %dynamic-update-slice), channel_id=1, replica_groups=mesh['row'=4,'col'=32] {'row','col'}, use_global_device_ids=true, to_apply=%add | all-reduce | flops 1024 | bytes 8192
  107.9 0.6 reduce_sum.49
  109.2 0.2 convert_reduce_fusion.2
  109.3 0.0 all-to-all-done.2
  109.3 0.2 convert_reduce_fusion.1
  109.5 0.7 broadcast_in_dim.8
  110.2 4.2 %all-to-all-start.4 = ((f32[4,1,4096]{2,1,0:T(1,128)}), f32[4,1,4096]{2,1,0:T(1,128)S(1)}, u32[]{:S(2)}, u32[]{:S(2)}) async-start(f32[4,1,4096]{2,1,0:T(1,128)} %broadcast_in_dim.8), calls=%async_computation.4 | async-start | bytes 131072 | tf_op jit(solution)/shard_map/all_to_all | solution.py:15
  114.4 0.0 all-gather.2.cloned.1.call-start
  114.4 0.1 dynamic-slice_subtract_fusion
  114.5 4.7 %all-to-all-done.4 = f32[4,1,4096]{2,1,0:T(1,128)S(1)} async-done(((f32[4,1,4096]{2,1,0:T(1,128)}), f32[4,1,4096]{2,1,0:T(1,128)S(1)}, u32[]{:S(2)}, u32[]{:S(2)}) %all-to-all-start.4) | async-done | bytes 65568 | tf_op jit(solution)/shard_map/all_to_all | solution.py:15
  119.2 0.1 reduce_sum.48
  119.2 0.6 fusion.9
  119.8 1.5 pad_maximum_fusion
  121.4 0.0 all-gather.2.cloned.1.call-update
  121.4 0.8 slice.9
  122.3 8.0 %all_to_all.54 = bf16[8,4,1024]{2,0,1:T(8,128)(2,1)S(1)} all-to-all(bf16[8,4,1024]{2,0,1:T(8,128)(2,1)S(1)} %bitcast.45), channel_id=1, replica_groups=mesh['row'=4,'col'=32] {'row'}, dimensions={1} | all-to-all | bytes 131072 | tf_op jit(solution)/shard_map/all_to_all | solution.py:70
  130.2 0.2 broadcast_in_dim.7
  130.5 31.3 %all_to_all.55 = bf16[32,32,1024]{2,1,0:T(8,128)(2,1)S(1)} all-to-all(bf16[32,32,1024]{2,1,0:T(8,128)(2,1)S(1)} %broadcast_in_dim.7), channel_id=1, replica_groups=mesh['row'=4,'col'=32] {'col'}, dimensions={0} | all-to-all | bytes 4194304 | tf_op jit(solution)/shard_map/all_to_all | solution.py:15
  161.8 0.4 convert_reduce_fusion
  162.2 0.6 fusion.10
  162.8 0.2 copy.7
  163.0 41.1 %all-gather.2.cloned.1.call-done = bf16[1024,4096]{1,0:T(8,128)(2,1)} async-done(((bf16[256,4096]{1,0:T(8,128)(2,1)}), bf16[1024,4096]{1,0:T(8,128)(2,1)}) %all-gather.2.cloned.1.call-update) | async-done | bytes 8388624 | tf_op jit(solution)/shard_map/all_gather | solution.py:42
  204.0 0.0 copy-start
  204.0 9.2 %convolution_multiply_fusion = f32[1024,2048]{1,0:T(8,128)} fusion(bf16[1024,1024]{1,0:T(8,128)(2,1)S(1)} %bitcast.41, bf16[1024,4096]{1,0:T(8,128)(2,1)} %all-gather.2.cloned.1.call-done), kind=kOutput, calls=%fused_computation.2 | convolution fusion | flops 4297064448 | bytes 14680064 | tf_op jit(solution)/shard_map/dot_general | solution.py:46
  213.2 0.0 copy-done
  213.2 6.9 %convolution_multiply_fusion.1 = f32[1024,2048]{1,0:T(8,128)} fusion(bf16[1024,1024]{1,0:T(8,128)(2,1)S(1)} %bitcast.42, bf16[1024,4096]{1,0:T(8,128)(2,1)S(1)} %copy-done), kind=kOutput, calls=%fused_computation.3 | convolution fusion | flops 4297064448 | bytes 14680064 | tf_op jit(solution)/shard_map/dot_general | solution.py:46
  (4 shorter events, 0.0 us)
Async XLA Ops:
  7.2 29.4 %copy-start.1 = (f32[8]{0:T(128)S(1)}, f32[8]{0:T(128)}, u32[]{:S(2)}) copy-start(f32[8]{0:T(128)} %param.5) | copy-start | bytes 100
  31.6 77.7 %all-to-all-start.2 = ((bf16[8,32,2048]{2,0,1:T(8,128)(2,1)}), bf16[8,32,2048]{2,0,1:T(8,128)(2,1)S(1)}, u32[]{:S(2)}, u32[]{:S(2)}) async-start(bf16[8,32,2048]{2,0,1:T(8,128)(2,1)} %bitcast.6), calls=%async_computation.2 | async-start | bytes 2097152 | tf_op jit(solution)/shard_map/all_to_all | solution.py:88
  110.2 9.0 %all-to-all-start.4 = ((f32[4,1,4096]{2,1,0:T(1,128)}), f32[4,1,4096]{2,1,0:T(1,128)S(1)}, u32[]{:S(2)}, u32[]{:S(2)}) async-start(f32[4,1,4096]{2,1,0:T(1,128)} %broadcast_in_dim.8), calls=%async_computation.4 | async-start | bytes 131072 | tf_op jit(solution)/shard_map/all_to_all | solution.py:15
  114.4 89.6 %all-gather.2.cloned.1.call-start = ((), (), s32[]{:S(2)}) async-start(), calls=%async_computation.5 | async-start | bytes 10485760 | tf_op jit(solution)/shard_map/all_gather | solution.py:42
  204.0 9.2 %copy-start = (bf16[1024,4096]{1,0:T(8,128)(2,1)S(1)}, bf16[1024,4096]{1,0:T(8,128)(2,1)}, u32[]{:S(2)}) copy-start(bf16[1024,4096]{1,0:T(8,128)(2,1)} %all-gather.2.cloned.1.call-done) | copy-start | bytes 25165828
Sparse Core Ops, SparseCore 0:
  121.5 82.4 all-gather.1
where the time goes:
time: 228 us; the launch traced here: 227 us
  blocking collectives  135 us (59%)
  waiting for transfers between devices  45.8 us (20%)
  matrix products  16.1 us (7%)
  between operations  14.8 us (6%)
  starting transfers between devices  9.12 us (4%)
  other arithmetic  4.22 us (2%)
    unnamed x1, blocking collectives  71.1 us
    all_gather x1, waiting for transfers between devices, in_one_piece(): lax.all_gather(both, axis, axis=dim, tiled=True)  41.1 us
    all_to_all x1, blocking collectives, from_everyone(): lax.all_to_all(jnp.broadcast_to(shard[None], (count, *shard.shape)), axis...  31.3 us
    all_to_all x1, blocking collectives, body(): lax.all_to_all(moving[1], 'col', split_axis=1, concat_axis=0, tiled=True)  24.4 us
    dot_general x2, matrix products, contract(): lax.dot_general(row_block, other, (((0,), (0,)), ((), ())), preferred_ele...  16.1 us
    all_to_all x1, blocking collectives, fetch_rows(): lax.all_to_all(source, 'row', split_axis=1, concat_axis=0, tiled=True)  7.98 us
    all_to_all x1, starting transfers between devices, body(): lax.all_to_all(moving[0], 'col', split_axis=1, concat_axis=0, tiled=True)  4.92 us
    all_to_all x1, waiting for transfers between devices, from_everyone(): lax.all_to_all(jnp.broadcast_to(shard[None], (count, *shard.shape)), axis...  4.69 us
  transfers between devices with their start and end apart: 3, of which 2 were waited for; matrix products, arithmetic and copies ran while one was open for 1% of the time, Pallas kernels for 0%

commit v1 on v0

v1 whole, which is shorter than its diff:
```python
import functools

import jax
import jax.numpy as jnp
from jax import lax
from jax.experimental import pallas as pl
from jax.experimental.pallas import tpu as pltpu
from jax.sharding import PartitionSpec as P

MESH = pl.DeviceIdType.MESH
LANES = 128
WIDTH = 128
TAIL = 4
F32 = jnp.float32
BF16 = jnp.bfloat16


def place():
    row, col = lax.axis_index("row"), lax.axis_index("col")
    x, y = (col // 4) % 4, col % 4
    return x, y, (row // 2) * 2 + col // 16, row % 2


def device(x, y, z, core):
    return {"row": (z // 2) * 2 + core, "col": (z % 2) * 16 + x * 4 + y}


def send(src, dst, send_sem, recv_sem, target):
    pltpu.make_async_remote_copy(
        src, dst, send_sem, recv_sem, device_id=device(*target), device_id_type=MESH
    ).start()


def keep(src, dst, sem):
    pltpu.make_async_copy(src, dst, sem).start()


def await_bytes(ref, sem):
    pltpu.make_async_copy(ref, ref, sem).wait()


def multiply(k, tiles, row_t, weight, mixed, store):
    total = 1024
    width = tiles.shape[-1]

    def add_up(i, sums):
        core, y = i // 4, i % 4
        return tuple(
            s + tiles[k, core, y, :, a].astype(F32).reshape(16, 8, width).sum(axis=0)
            for a, s in enumerate(sums)
        )

    zero = jnp.zeros((8, width), F32)
    sums = lax.fori_loop(0, 8, add_up, (zero, zero), unroll=True)
    means = [s.sum(axis=0, keepdims=True) / total for s in sums]

    def centre(i, _):
        core, y = i // 4, i % 4
        offset = tiles[k, core, y, :, 0].astype(F32).reshape(128, width) - means[0]
        grad = tiles[k, core, y, :, 1].astype(F32).reshape(128, width) - means[1]
        rows = pl.ds(pl.multiple_of(i * 128, 128), 128)
        mixed[rows, 0:width] = offset.astype(BF16)
        mixed[rows, width : 2 * width] = (weight[rows, :] * offset + grad).astype(BF16)
        return 0

    lax.fori_loop(0, 8, centre, 0)

    def part(i, _):
        rows = pl.ds(pl.multiple_of(i * 256, 256), 256)
        store(rows, jnp.dot(row_t[rows, :], mixed[...], preferred_element_type=F32) / total)
        return 0

    lax.fori_loop(0, 4, part, 0)


def exchange(
    derivs, grads, energy, tiles, row_t, weight, done,
    zb, xb, r0, ra, rb, ez, ex, ey, mixed,
    s_z, s_x, s_y, s_c, s_r, s_e, z_sem, x_sem, y_sem, c_sem, r_sem, e_sem,
):
    x, y, z, core = place()
    chunks = tiles.shape[0]
    quarter = chunks // 4
    early = done.shape[0]
    mates = [(x, y, (z + d) % 4, core) for d in (2, 1, 3)]
    others = [(x, y, (z + d) % 4, 1 - core) for d in (0, 2, 1, 3)]
    along_x = [((x + d) % 4, y, z, core) for d in (2, 1, 3)]
    along_y = [(x, (y + d) % 4, z, core) for d in (2, 1, 3)]
    partner = (x, y, z, 1 - core)

    barrier = pltpu.get_barrier_semaphore()
    for peer in mates + others + along_x + along_y:
        pl.semaphore_signal(barrier, 1, device_id=device(*peer), device_id_type=MESH)
    pl.semaphore_wait(barrier, 13)

    for group, sem in ((mates, 0), (others, 1)):
        for peer in group:
            block = derivs.at[0, 0, peer[2] // 2, pl.ds(peer[3] * 2, 2)]
            send(block, r0.at[core, z], s_r.at[sem], r_sem.at[0], peer)
    keep(derivs.at[0, 0, z // 2, pl.ds(core * 2, 2)], r0.at[core, z], r_sem.at[0])
    for peer in mates:
        send(energy, ez.at[z], s_e.at[0], e_sem.at[0], peer)
    keep(energy, ez.at[z], e_sem.at[0])

    @pl.loop(0, chunks)
    def _(k):
        for a, source in enumerate((derivs, grads)):
            for peer in mates:
                block = source.at[peer[2] % 2, :, :, k // quarter, k % quarter]
                send(block, zb.at[k, :, :, a, z], s_z, z_sem.at[k], peer)
            block = source.at[z % 2, :, :, k // quarter, k % quarter]
            keep(block, zb.at[k, :, :, a, z], z_sem.at[k])

    await_bytes(r0, r_sem.at[0])
    for peer in along_x:
        send(r0.at[:, :, 0], ra.at[y, x], s_r.at[2], r_sem.at[1], peer)
    keep(r0.at[:, :, 0], ra.at[y, x], r_sem.at[1])
    for peer in along_y:
        send(r0.at[:, :, 1], rb.at[x, y], s_r.at[3], r_sem.at[2], peer)
    keep(r0.at[:, :, 1], rb.at[x, y], r_sem.at[2])
    await_bytes(ez, e_sem.at[0])
    for peer in along_x:
        send(ez, ex.at[x], s_e.at[1], e_sem.at[1], peer)
    keep(ez, ex.at[x], e_sem.at[1])
    await_bytes(ra.at[y], r_sem.at[1])
    for peer in along_y:
        send(ra.at[y], ra.at[y], s_r.at[4], r_sem.at[3], peer)
    await_bytes(rb.at[x], r_sem.at[2])
    for peer in along_x:
        send(rb.at[x], rb.at[x], s_r.at[5], r_sem.at[4], peer)
    await_bytes(ex, e_sem.at[1])
    for peer in along_y:
        send(ex, ey.at[core, y], s_e.at[2], e_sem.at[2], peer)
    keep(ex, ey.at[core, y], e_sem.at[2])

    def to_x(k):
        await_bytes(zb.at[k], z_sem.at[k])
        for peer in along_x:
            send(zb.at[k, peer[0]], xb.at[k, :, x], s_x, x_sem.at[k], peer)
        keep(zb.at[k, x], xb.at[k, :, x], x_sem.at[k])

    def to_y(k):
        await_bytes(xb.at[k], x_sem.at[k])
        for peer in along_y:
            send(xb.at[k, peer[1]], tiles.at[k, core, y], s_y, y_sem.at[k], peer)
        keep(xb.at[k, y], tiles.at[k, core, y], y_sem.at[k])

    def to_partner(k):
        await_bytes(tiles.at[k, core], y_sem.at[k])
        send(tiles.at[k, core], tiles.at[k, core], s_c, c_sem.at[k], partner)

    def finish(k):
        await_bytes(tiles.at[k, 1 - core], c_sem.at[k])

        def store(rows, value):
            done[k, rows, :] = value

        multiply(k, tiles, row_t, weight, mixed, store)

    first = 5

    @pl.loop(0, first)
    def _(k):
        to_x(k)

        @pl.when(k >= 1)
        def _():
            to_y(k - 1)

        @pl.when(k >= 2)
        def _():
            to_partner(k - 2)

    await_bytes(ey.at[core], e_sem.at[2])
    send(ey.at[core], ey.at[core], s_e.at[3], e_sem.at[3], partner)

    await_bytes(ra.at[0:3], r_sem.at[3])
    await_bytes(rb.at[0:3], r_sem.at[4])

    @pl.loop(0, quarter)
    def _(c):
        for half, source in enumerate((ra, rb)):
            blocks = []
            for i in range(8):
                if half == 0:
                    block = source[i % 4, :, i // 4, :, c]
                else:
                    block = source[:, i % 4, i // 4, :, c]
                blocks.append(block.astype(F32).reshape(128, LANES))
            total = sum(b.reshape(16, 8, LANES).sum(axis=0) for b in blocks)
            mean = total.sum(axis=0, keepdims=True) / 1024
            rows = pl.ds(pl.multiple_of((half * quarter + c) * LANES, LANES), LANES)
            for i, block in enumerate(blocks):
                row_t[rows, i * 128 : (i + 1) * 128] = (block - mean).T.astype(BF16)

    await_bytes(ey.at[1 - core], e_sem.at[3])
    every = ey[...].reshape(1024, LANES)
    mean_energy = every.reshape(128, 8, LANES).sum(axis=0).sum(axis=0, keepdims=True) / 1024
    weight[...] = every - mean_energy

    @pl.loop(first, chunks)
    def _(k):
        to_x(k)
        to_y(k - 1)
        to_partner(k - 2)
        finish(k - first)

    to_y(chunks - 1)
    to_partner(chunks - 2)
    if chunks - first < early:
        finish(chunks - first)
    to_partner(chunks - 1)
    if chunks - first + 1 < early:
        pl.loop(chunks - first + 1, early)(finish)
    pl.loop(early, chunks)(lambda k: await_bytes(tiles.at[k, 1 - core], c_sem.at[k]))

    await_bytes(zb.at[:, 0:3], s_z)
    await_bytes(xb.at[:, 0:3], s_x)
    await_bytes(tiles.at[:, 0, 0:3], s_y)
    await_bytes(tiles.at[:, 0], s_c)
    await_bytes(r0.at[0, 0:3], s_r.at[0])
    await_bytes(r0.at[0], s_r.at[1])
    await_bytes(ra.at[0, 0:3], s_r.at[2])
    await_bytes(rb.at[0, 0:3], s_r.at[3])
    await_bytes(ra.at[0:3], s_r.at[4])
    await_bytes(rb.at[0:3], s_r.at[5])
    await_bytes(ez.at[0:3], s_e.at[0])
    await_bytes(ex.at[0:3], s_e.at[1])
    await_bytes(ey.at[0, 0:3], s_e.at[2])
    await_bytes(ey.at[0], s_e.at[3])


def write(tiles, row_t, weight, done, corr, hamil, late, mixed, sem):
    chunks, early = tiles.shape[0], done.shape[0]
    outs = (corr, hamil)

    def put(source, k):
        for a, out in enumerate(outs):
            columns = pl.ds(pl.multiple_of(k * LANES, LANES), LANES)
            keep(source.at[:, a * LANES : (a + 1) * LANES], out.at[:, columns], sem.at[a])

    pl.loop(0, early)(lambda k: put(done.at[k], k))

    @pl.loop(early, chunks)
    def _(k):
        def store(rows, value):
            late[k - early, rows, :] = value

        multiply(k, tiles, row_t, weight, mixed, store)
        put(late.at[k - early], k)

    for a, out in enumerate(outs):
        await_bytes(out, sem.at[a])


def body(derivs, grads, energies):
    chunks = 2048 // WIDTH
    early = chunks - TAIL
    quarter = chunks // 4

    def view(a):
        return a.reshape(8, 2, 4, 4, 4, quarter, WIDTH).transpose(1, 2, 3, 4, 5, 0, 6)

    energy = jnp.broadcast_to(energies[:, None], (8, LANES))
    hbm = pl.BlockSpec(memory_space=pl.ANY)
    vmem = pl.BlockSpec(memory_space=pltpu.VMEM)
    dma = pltpu.SemaphoreType.DMA
    tiles, row_t, weight, done = pl.pallas_call(
        exchange,
        out_shape=(
            pltpu.VMEM((chunks, 2, 4, 4, 2, 4, 8, WIDTH), BF16),
            pltpu.VMEM((1024, 1024), BF16),
            pltpu.VMEM((1024, LANES), F32),
            pltpu.VMEM((early, 1024, 2 * WIDTH), F32),
        ),
        in_specs=[hbm, hbm, vmem],
        out_specs=(vmem,) * 4,
        scratch_shapes=[
            pltpu.VMEM((chunks, 4, 4, 2, 4, 8, WIDTH), BF16),
            pltpu.VMEM((chunks, 4, 4, 2, 4, 8, WIDTH), BF16),
            pltpu.VMEM((2, 4, 2, quarter, 8, WIDTH), BF16),
            pltpu.VMEM((4, 4, 2, 4, quarter, 8, WIDTH), BF16),
            pltpu.VMEM((4, 4, 2, 4, quarter, 8, WIDTH), BF16),
            pltpu.VMEM((4, 8, LANES), F32),
            pltpu.VMEM((4, 4, 8, LANES), F32),
            pltpu.VMEM((2, 4, 4, 4, 8, LANES), F32),
            pltpu.VMEM((1024, 2 * WIDTH), BF16),
            dma, dma, dma, dma, dma((6,)), dma((4,)),
            dma((chunks,)), dma((chunks,)), dma((chunks,)), dma((chunks,)), dma((5,)), dma((4,)),
        ],
        compiler_params=pltpu.CompilerParams(
            collective_id=0, has_side_effects=True, vmem_limit_bytes=20 << 20
        ),
        name="exchange",
    )(view(derivs), view(grads), energy)
    out = jax.ShapeDtypeStruct((1024, 2048), F32)
    return pl.pallas_call(
        write,
        out_shape=(out, out),
        in_specs=[vmem] * 4,
        out_specs=(hbm, hbm),
        scratch_shapes=[
            pltpu.VMEM((TAIL, 1024, 2 * WIDTH), F32),
            pltpu.VMEM((1024, 2 * WIDTH), BF16),
            dma((2,)),
        ],
        compiler_params=pltpu.CompilerParams(vmem_limit_bytes=8 << 20),
        name="write",
    )(tiles, row_t, weight, done)


def solution(mesh):
    placed = (P(("row", "col"), None), P(("row", "col"), None), P(("row", "col")))
    return jax.shard_map(
        body,
        mesh=mesh,
        in_specs=placed,
        out_specs=(P("row", "col"), P("row", "col")),
        check_vma=False,
    )
```

time: 228 us -> 110 us (0.48)
  blocking collectives: 135 us -> 0 us
  Pallas kernels: 0 us -> 106 us
  waiting for transfers between devices: 45.8 us -> 0 us
  matrix products: 16.1 us -> 0 us
  between operations: 14.8 us -> 0.64 us
  starting transfers between devices: 9.12 us -> 0 us
  other arithmetic: 4.22 us -> 0 us
    pallas_call x0 -> x2, Pallas kernels: none -> 106 us  [the longest x1 98.8 us: body(): pl.pallas_call(exchange, out_shape=(pltpu.VMEM((chunks, 2, 4, 4, 2, 4, 8,...]
    unnamed x1 -> x0, blocking collectives: 71.1 us -> none
    all_to_all x3 -> x0, blocking collectives: 63.7 us -> none  [the longest x1 31.3 us: from_everyone(): lax.all_to_all(jnp.broadcast_to(shard[None], (count, *shard.shape)), axis...]
    all_gather x1 -> x0, waiting for transfers between devices: 41.1 us -> none  [in_one_piece(): lax.all_gather(both, axis, axis=dim, tiled=True)]
    dot_general x2 -> x0, matrix products: 16.1 us -> none  [contract(): lax.dot_general(row_block, other, (((0,), (0,)), ((), ())), preferred_ele...]
    all_to_all x2 -> x0, starting transfers between devices: 9.12 us -> none  [the longest x1 4.92 us: body(): lax.all_to_all(moving[0], 'col', split_axis=1, concat_axis=0, tiled=True)]
    all_to_all x2 -> x0, waiting for transfers between devices: 4.69 us -> none  [the longest x1 4.69 us: from_everyone(): lax.all_to_all(jnp.broadcast_to(shard[None], (count, *shard.shape)), axis...]
  transfers between devices with their start and end apart: 3 -> 0, of which waited for: 2 -> 0; matrix products, arithmetic and copies ran while one was open for 1% -> 0% of each run, Pallas kernels for 0% -> 0%
where the time goes in v1:
time: 110 us
  Pallas kernels  106 us (96%)
  local copies, waits for them, and re-layouts  3.17 us (3%)
    pallas_call x1, Pallas kernels, body(): pl.pallas_call(exchange, out_shape=(pltpu.VMEM((chunks, 2, 4, 4, 2, 4, 8,...  98.8 us
    pallas_call x1, Pallas kernels, body(): pl.pallas_call(write, out_shape=(out, out), in_specs=[vmem] * 4, out_spec...  7.28 us
    unnamed x4, local copies, waits for them, and re-layouts  2.45 us

profile of v1, /device:TPU:1, one launch (start us, length us, event | category | flops | bytes accessed | tf_op | source)
XLA Modules:
  0.0 109.9 jit_solution(9591775900304241417)
XLA Ops:
  0.6 0.7 broadcast_in_dim.2.energy
  1.4 0.0 copy-start
  1.4 1.2 %copy-done = bf16[8,65536]{1,0:T(8,128)(2,1)S(1)} copy-done((bf16[8,65536]{1,0:T(8,128)(2,1)S(1)}, bf16[8,65536]{1,0:T(8,128)(2,1)}, u32[]{:S(2)}) %copy-start) | copy-done | bytes 1048600
  2.6 0.0 copy-start.1
  2.6 1.2 %copy-done.1 = bf16[8,65536]{1,0:T(8,128)(2,1)S(1)} copy-done((bf16[8,65536]{1,0:T(8,128)(2,1)S(1)}, bf16[8,65536]{1,0:T(8,128)(2,1)}, u32[]{:S(2)}) %copy-start.1) | copy-done | bytes 1048600
  3.8 98.8 %exchange.1 = (bf16[16,2,4,4,2,4,8,128]{7,6,5,4,3,2,1,0:T(8,128)(2,1)S(1)}, bf16[1024,1024]{1,0:T(8,128)(2,1)S(1)}, f32[1024,128]{1,0:T(8,128)S(1)}, f32[12,1024,256]{2,1,0:T(8,128)S(1)}) custom-call(bf16[2,4,4,4,4,8,128]{6,5,4,3,2,1,0:T(8,128)(2,1)S(1)} %bitcast.6, bf16[2,4,4,4,4,8,128]{6,5,4,3,2,1,0:T(8,128)(2,1)S(1)} %bitcast.7, ...), custom_call_target="tpu_custom_call" | custom-call | tf_op jit(solution)/shard_map/exchange/pallas_call | solution.py:268
  102.6 7.3 %write.1 = (f32[1024,2048]{1,0:T(8,128)}, f32[1024,2048]{1,0:T(8,128)}) custom-call(bf16[16,2,4,4,2,4,8,128]{7,6,5,4,3,2,1,0:T(8,128)(2,1)S(1)} %get-tuple-element.6.tiles, bf16[1024,1024]{1,0:T(8,128)(2,1)S(1)} %get-tuple-element.7.row_t, f32[1024,128]{1,0:T(8,128)S(1)} %get-tuple-element.8.weight, f32[12,1024,256]{2,1,0:T(8,128)S(1)} %get-tuple-element.9.done), custom_call_target="tpu_custom_call" | custom-call | tf_op jit(solution)/shard_map/write/pallas_call | solution.py:297
Async XLA Ops:
  1.4 1.2 %copy-start = (bf16[8,65536]{1,0:T(8,128)(2,1)S(1)}, bf16[8,65536]{1,0:T(8,128)(2,1)}, u32[]{:S(2)}) copy-start(bf16[8,65536]{1,0:T(8,128)(2,1)} %param.3) | copy-start | bytes 3145732
  2.6 1.2 %copy-start.1 = (bf16[8,65536]{1,0:T(8,128)(2,1)S(1)}, bf16[8,65536]{1,0:T(8,128)(2,1)}, u32[]{:S(2)}) copy-start(bf16[8,65536]{1,0:T(8,128)(2,1)} %param.4) | copy-start | bytes 3145732

commit v2 on v1

v2 whole, which is shorter than its diff:
```python
import functools

import jax
import jax.numpy as jnp
from jax import lax
from jax.experimental import pallas as pl
from jax.experimental.pallas import tpu as pltpu
from jax.sharding import PartitionSpec as P

MESH = pl.DeviceIdType.MESH
LANES = 128
WIDTH = 128
AHEAD = 3
LAG_Y = 2
LAG_Z = 3
SLAB_STEP = 3
FIRST = 11
TAIL = 2
F32 = jnp.float32
BF16 = jnp.bfloat16


def place():
    row, col = lax.axis_index("row"), lax.axis_index("col")
    x, y = (col // 4) % 4, col % 4
    return x, y, (row // 2) * 2 + col // 16, row % 2


def device(x, y, z, core):
    return {"row": (z // 2) * 2 + core, "col": (z % 2) * 16 + x * 4 + y}


def send(src, dst, send_sem, recv_sem, target):
    pltpu.make_async_remote_copy(
        src, dst, send_sem, recv_sem, device_id=device(*target), device_id_type=MESH
    ).start()


def keep(src, dst, sem):
    pltpu.make_async_copy(src, dst, sem).start()


def await_bytes(ref, sem):
    pltpu.make_async_copy(ref, ref, sem).wait()


def multiply(k, tiles, row_t, weight, mixed, store):
    total = 1024
    width = tiles.shape[-1]

    def add_up(i, sums):
        core, z = i // 4, i % 4
        return tuple(
            s + tiles[k, core, z, :, a].astype(F32).reshape(16, 8, width).sum(axis=0)
            for a, s in enumerate(sums)
        )

    zero = jnp.zeros((8, width), F32)
    sums = lax.fori_loop(0, 8, add_up, (zero, zero), unroll=True)
    means = [s.sum(axis=0, keepdims=True) / total for s in sums]

    def centre(i, _):
        core, z = i // 4, i % 4
        offset = tiles[k, core, z, :, 0].astype(F32).reshape(128, width) - means[0]
        grad = tiles[k, core, z, :, 1].astype(F32).reshape(128, width) - means[1]
        rows = pl.ds(pl.multiple_of(i * 128, 128), 128)
        mixed[rows, 0:width] = offset.astype(BF16)
        mixed[rows, width : 2 * width] = (weight[rows, :] * offset + grad).astype(BF16)
        return 0

    lax.fori_loop(0, 8, centre, 0)

    def part(i, _):
        rows = pl.ds(pl.multiple_of(i * 256, 256), 256)
        store(rows, jnp.dot(row_t[rows, :], mixed[...], preferred_element_type=F32) / total)
        return 0

    lax.fori_loop(0, 4, part, 0)


def exchange(
    derivs, grads, energies, tiles, row_t, weight, done,
    energy, xb, yb, r0, ra, rb, ez, ex, ey, mixed,
    s_x, s_y, s_z, s_c, s_r, s_e, x_sem, y_sem, z_sem, c_sem, r_sem, e_sem,
):
    x, y, z, core = place()
    chunks = tiles.shape[0]
    quarter = chunks // 4
    early = done.shape[0]
    mates = [(x, y, (z + d) % 4, core) for d in (2, 1, 3)]
    others = [(x, y, (z + d) % 4, 1 - core) for d in (0, 2, 1, 3)]
    along_x = [((x + d) % 4, y, z, core) for d in (2, 1, 3)]
    along_y = [(x, (y + d) % 4, z, core) for d in (2, 1, 3)]
    partner = (x, y, z, 1 - core)

    own = lax.broadcasted_iota(jnp.int32, (8, 8), 0) == lax.broadcasted_iota(jnp.int32, (8, 8), 1)
    column = jnp.where(own, energies[...], 0).sum(axis=1, keepdims=True)
    energy[...] = jnp.broadcast_to(column, (8, LANES))

    barrier = pltpu.get_barrier_semaphore()
    for peer in mates + others + along_x + along_y:
        pl.semaphore_signal(barrier, 1, device_id=device(*peer), device_id_type=MESH)
    pl.semaphore_wait(barrier, 13)

    @jax.named_scope("to_x")
    def to_x(k):
        for a, source in enumerate((derivs, grads)):
            for peer in along_x:
                block = source.at[:, peer[0], :, k // quarter, k % quarter]
                send(block, xb.at[k, :, :, a, x], s_x, x_sem.at[k], peer)
            block = source.at[:, x, :, k // quarter, k % quarter]
            keep(block, xb.at[k, :, :, a, x], x_sem.at[k])

    @jax.named_scope("to_y")
    def to_y(k):
        await_bytes(xb.at[k], x_sem.at[k])
        for peer in along_y:
            send(xb.at[k, :, peer[1]], yb.at[k, :, y], s_y, y_sem.at[k], peer)
        keep(xb.at[k, :, y], yb.at[k, :, y], y_sem.at[k])

    @jax.named_scope("to_z")
    def to_z(k):
        await_bytes(yb.at[k], y_sem.at[k])
        for peer in mates:
            send(yb.at[k, peer[2] % 2], tiles.at[k, core, z], s_z, z_sem.at[k], peer)
        keep(yb.at[k, z % 2], tiles.at[k, core, z], z_sem.at[k])

    @jax.named_scope("to_partner")
    def to_partner(k):
        await_bytes(tiles.at[k, core], z_sem.at[k])
        send(tiles.at[k, core], tiles.at[k, core], s_c, c_sem.at[k], partner)

    @jax.named_scope("finish")
    def finish(k):
        await_bytes(tiles.at[k, 1 - core], c_sem.at[k])

        def store(rows, value):
            done[k, rows, :] = value

        multiply(k, tiles, row_t, weight, mixed, store)

    def when(condition, stage, k):
        pl.when(condition)(functools.partial(stage, k))

    def finished(i):
        return jnp.clip(jnp.minimum(2 * (i + 1 - FIRST), i - LAG_Y - LAG_Z), 0, early)

    def step(i):
        when(i + AHEAD < chunks, to_x, i + AHEAD)
        when(i < chunks, to_y, i)
        when((i >= LAG_Y) & (i < chunks + LAG_Y), to_z, i - LAG_Y)
        late = i - LAG_Y - LAG_Z
        when((late >= 0) & (late < chunks), to_partner, late)

    to_x(0)
    for group, sem in ((mates, 0), (others, 1)):
        for peer in group:
            block = derivs.at[0, 0, peer[2] // 2, pl.ds(peer[3] * 2, 2)]
            send(block, r0.at[core, z], s_r.at[sem], r_sem.at[0], peer)
    keep(derivs.at[0, 0, z // 2, pl.ds(core * 2, 2)], r0.at[core, z], r_sem.at[0])
    for peer in mates:
        send(energy, ez.at[z], s_e.at[0], e_sem.at[0], peer)
    keep(energy, ez.at[z], e_sem.at[0])
    for k in range(1, AHEAD):
        to_x(k)

    step(0)
    with jax.named_scope("r1"):
        await_bytes(r0, r_sem.at[0])
        for peer in along_x:
            send(r0.at[:, :, 0], ra.at[y, x], s_r.at[2], r_sem.at[1], peer)
        keep(r0.at[:, :, 0], ra.at[y, x], r_sem.at[1])
        for peer in along_y:
            send(r0.at[:, :, 1], rb.at[x, y], s_r.at[3], r_sem.at[2], peer)
        keep(r0.at[:, :, 1], rb.at[x, y], r_sem.at[2])
        await_bytes(ez, e_sem.at[0])
        for peer in along_x:
            send(ez, ex.at[x], s_e.at[1], e_sem.at[1], peer)
        keep(ez, ex.at[x], e_sem.at[1])
    pl.loop(1, SLAB_STEP)(step)
    with jax.named_scope("r2"):
        await_bytes(ra.at[y], r_sem.at[1])
        await_bytes(rb.at[x], r_sem.at[2])
        await_bytes(ex, e_sem.at[1])

    @pl.loop(SLAB_STEP, SLAB_STEP + 4)
    def _(i):
        step(i)
        for side in range(2):
            part = (side, i - SLAB_STEP)
            for peer in along_y:
                send(ra.at[(y, slice(None), *part)], ra.at[(y, slice(None), *part)], s_r.at[4], r_sem.at[3], peer)
            for peer in along_x:
                send(rb.at[(x, slice(None), *part)], rb.at[(x, slice(None), *part)], s_r.at[5], r_sem.at[4], peer)

    for peer in along_y:
        send(ex, ey.at[core, y], s_e.at[2], e_sem.at[2], peer)
    keep(ex, ey.at[core, y], e_sem.at[2])
    pl.loop(SLAB_STEP + 4, FIRST - 1)(step)
    with jax.named_scope("e"):
        await_bytes(ey.at[core], e_sem.at[2])
    send(ey.at[core], ey.at[core], s_e.at[3], e_sem.at[3], partner)
    step(FIRST - 1)

    with jax.named_scope("r3"):
        await_bytes(ra.at[0:3], r_sem.at[3])
        await_bytes(rb.at[0:3], r_sem.at[4])

    @pl.loop(0, quarter)
    @jax.named_scope("prep")
    def _(c):
        for half, source in enumerate((ra, rb)):
            blocks = []
            for i in range(8):
                block = source[:, :, i // 4, i % 4, c].astype(F32)
                if half == 1:
                    block = jnp.stack([block[:, j] for j in range(4)])
                blocks.append(block.reshape(128, LANES))
            total = sum(b.reshape(16, 8, LANES).sum(axis=0) for b in blocks)
            mean = total.sum(axis=0, keepdims=True) / 1024
            rows = pl.ds(pl.multiple_of((half * quarter + c) * LANES, LANES), LANES)
            for i, block in enumerate(blocks):
                row_t[rows, i * 128 : (i + 1) * 128] = (block - mean).T.astype(BF16)

    await_bytes(ey.at[1 - core], e_sem.at[3])
    mean_energy = ey[...].reshape(128, 8, LANES).sum(axis=0).sum(axis=0, keepdims=True) / 1024
    for i in range(8):
        every = ey[i // 4, :, :, i % 4].reshape(128, LANES)
        weight[i * 128 : (i + 1) * 128, :] = every - mean_energy

    @pl.loop(FIRST, chunks + LAG_Y + LAG_Z)
    def _(i):
        step(i)
        pl.loop(finished(i - 1), finished(i))(finish)

    pl.loop(finished(chunks + LAG_Y + LAG_Z - 1), early)(finish)
    pl.loop(early, chunks)(lambda k: await_bytes(tiles.at[k, 1 - core], c_sem.at[k]))

    await_bytes(xb.at[:, :, 0:3], s_x)
    await_bytes(yb.at[:, :, 0:3], s_y)
    await_bytes(tiles.at[:, 0, 0:3], s_z)
    await_bytes(tiles.at[:, 0], s_c)
    await_bytes(r0.at[0, 0:3], s_r.at[0])
    await_bytes(r0.at[0], s_r.at[1])
    await_bytes(ra.at[0, 0:3], s_r.at[2])
    await_bytes(rb.at[0, 0:3], s_r.at[3])
    await_bytes(ra.at[0:3], s_r.at[4])
    await_bytes(rb.at[0:3], s_r.at[5])
    await_bytes(ez.at[0:3], s_e.at[0])
    await_bytes(ex.at[0:3], s_e.at[1])
    await_bytes(ey.at[0, 0:3], s_e.at[2])
    await_bytes(ey.at[0], s_e.at[3])


def write(tiles, row_t, weight, done, corr, hamil, late, mixed, sem):
    chunks, early = tiles.shape[0], done.shape[0]
    outs = (corr, hamil)

    def put(source, k):
        for a, out in enumerate(outs):
            columns = pl.ds(pl.multiple_of(k * LANES, LANES), LANES)
            keep(source.at[:, a * LANES : (a + 1) * LANES], out.at[:, columns], sem.at[a])

    pl.loop(0, early)(lambda k: put(done.at[k], k))

    @pl.loop(early, chunks)
    def _(k):
        def store(rows, value):
            late[k - early, rows, :] = value

        multiply(k, tiles, row_t, weight, mixed, store)
        put(late.at[k - early], k)

    for a, out in enumerate(outs):
        await_bytes(out, sem.at[a])


def body(derivs, grads, energies):
    chunks = 2048 // WIDTH
    early = chunks - TAIL
    quarter = chunks // 4

    def view(a):
        a = a.reshape(8, 2, 4, 4, 4, quarter, WIDTH).transpose(1, 2, 3, 4, 5, 0, 6)
        return pltpu.with_memory_space_constraint(a, pltpu.HBM)

    hbm = pl.BlockSpec(memory_space=pltpu.HBM)
    vmem = pl.BlockSpec(memory_space=pltpu.VMEM)
    dma = pltpu.SemaphoreType.DMA
    tiles, row_t, weight, done = pl.pallas_call(
        exchange,
        out_shape=(
            pltpu.VMEM((chunks, 2, 4, 4, 2, 4, 8, WIDTH), BF16),
            pltpu.VMEM((1024, 1024), BF16),
            pltpu.VMEM((1024, LANES), F32),
            pltpu.VMEM((early, 1024, 2 * WIDTH), F32),
        ),
        in_specs=[hbm, hbm, vmem],
        out_specs=(vmem,) * 4,
        scratch_shapes=[
            pltpu.VMEM((8, LANES), F32),
            pltpu.VMEM((chunks, 2, 4, 2, 4, 8, WIDTH), BF16),
            pltpu.VMEM((chunks, 2, 4, 2, 4, 8, WIDTH), BF16),
            pltpu.VMEM((2, 4, 2, quarter, 8, WIDTH), BF16),
            pltpu.VMEM((4, 4, 2, 4, quarter, 8, WIDTH), BF16),
            pltpu.VMEM((4, 4, 2, 4, quarter, 8, WIDTH), BF16),
            pltpu.VMEM((4, 8, LANES), F32),
            pltpu.VMEM((4, 4, 8, LANES), F32),
            pltpu.VMEM((2, 4, 4, 4, 8, LANES), F32),
            pltpu.VMEM((1024, 2 * WIDTH), BF16),
            dma, dma, dma, dma, dma((6,)), dma((4,)),
            dma((chunks,)), dma((chunks,)), dma((chunks,)), dma((chunks,)), dma((5,)), dma((4,)),
        ],
        compiler_params=pltpu.CompilerParams(
            collective_id=0, has_side_effects=True, vmem_limit_bytes=20 << 20
        ),
        name="exchange",
    )(view(derivs), view(grads), energies.reshape(1, 8))
    out = jax.ShapeDtypeStruct((1024, 2048), F32)
    return pl.pallas_call(
        write,
        out_shape=(out, out),
        in_specs=[vmem] * 4,
        out_specs=(hbm, hbm),
        scratch_shapes=[
            pltpu.VMEM((TAIL, 1024, 2 * WIDTH), F32),
            pltpu.VMEM((1024, 2 * WIDTH), BF16),
            dma((2,)),
        ],
        compiler_params=pltpu.CompilerParams(vmem_limit_bytes=8 << 20),
        name="write",
    )(tiles, row_t, weight, done)


def solution(mesh):
    placed = (P(("row", "col"), None), P(("row", "col"), None), P(("row", "col")))
    return jax.shard_map(
        body,
        mesh=mesh,
        in_specs=placed,
        out_specs=(P("row", "col"), P("row", "col")),
        check_vma=False,
    )
```

time: 110 us -> 80.3 us (0.73)
  Pallas kernels: 106 us -> 78.9 us
  local copies, waits for them, and re-layouts: 3.17 us -> 0.65 us
    pallas_call x1, Pallas kernels: 98.8 us -> 73.1 us  [body(): pl.pallas_call(exchange, out_shape=(pltpu.VMEM((chunks, 2, 4, 4, 2, 4, 8,...]
    unnamed x4 -> x2, local copies, waits for them, and re-layouts: 2.45 us -> 0.65 us
    pallas_call x1, Pallas kernels: 7.28 us -> 5.81 us  [body(): pl.pallas_call(write, out_shape=(out, out), in_specs=[vmem] * 4, out_spec...]
where the time goes in v2:
time: 80.3 us; the launch traced here: 80.2 us
  Pallas kernels  78.9 us (98%)
    pallas_call x1, Pallas kernels, body(): pl.pallas_call(exchange, out_shape=(pltpu.VMEM((chunks, 2, 4, 4, 2, 4, 8,...  73.1 us
    pallas_call x1, Pallas kernels, body(): pl.pallas_call(write, out_shape=(out, out), in_specs=[vmem] * 4, out_spec...  5.81 us

profile of v2, /device:TPU:1, one launch (start us, length us, event | category | flops | bytes accessed | tf_op | source)
XLA Modules:
  0.0 80.2 jit_solution(5821532234627622638)
XLA Ops:
  0.6 0.0 copy-start
  0.6 0.6 copy-done
  1.3 73.1 %exchange.1 = (bf16[16,2,4,4,2,4,8,128]{7,6,5,4,3,2,1,0:T(8,128)(2,1)S(1)}, bf16[1024,1024]{1,0:T(8,128)(2,1)S(1)}, f32[1024,128]{1,0:T(8,128)S(1)}, f32[14,1024,256]{2,1,0:T(8,128)S(1)}) custom-call(bf16[2,4,4,4,4,8,128]{6,5,4,3,2,1,0:T(8,128)(2,1)} %bitcast.8, bf16[2,4,4,4,4,8,128]{6,5,4,3,2,1,0:T(8,128)(2,1)} %bitcast.9, f32[1,8]{1,0:T(1,128)S(1)} %bitcast.7), custom_call_target="tpu_custom_call" | custom-call | tf_op jit(solution)/shard_map/exchange/pallas_call | solution.py:290
  74.4 5.8 %write.1 = (f32[1024,2048]{1,0:T(8,128)}, f32[1024,2048]{1,0:T(8,128)}) custom-call(bf16[16,2,4,4,2,4,8,128]{7,6,5,4,3,2,1,0:T(8,128)(2,1)S(1)} %get-tuple-element.6.tiles, bf16[1024,1024]{1,0:T(8,128)(2,1)S(1)} %get-tuple-element.7.row_t, f32[1024,128]{1,0:T(8,128)S(1)} %get-tuple-element.8.weight, f32[14,1024,256]{2,1,0:T(8,128)S(1)} %get-tuple-element.9.done), custom_call_target="tpu_custom_call" | custom-call | tf_op jit(solution)/shard_map/write/pallas_call | solution.py:320
Async XLA Ops:
  0.6 0.7 copy-start

commit v3 on v2

--- a/solution.py
+++ b/solution.py
@@ -10,12 +10,20 @@
 MESH = pl.DeviceIdType.MESH
 LANES = 128
 WIDTH = 128
+EARLY_Z = 1
+F_STEP = 3
+F_LAG = 2
+AT_ONCE = 2
 AHEAD = 3
 LAG_Y = 2
 LAG_Z = 3
 SLAB_STEP = 3
-FIRST = 11
-TAIL = 2
+FIRST = 13
+PIECES = 1
+RELAY_LAG = 2
+PACE = 3
+BLOCK = 256
+TAIL = 4
 F32 = jnp.float32
 BF16 = jnp.bfloat16
 
@@ -47,41 +55,28 @@
 def multiply(k, tiles, row_t, weight, mixed, store):
     total = 1024
     width = tiles.shape[-1]
-
-    def add_up(i, sums):
-        core, z = i // 4, i % 4
-        return tuple(
-            s + tiles[k, core, z, :, a].astype(F32).reshape(16, 8, width).sum(axis=0)
+    sums = [jnp.zeros((8, width), F32)] * 2
+    for i in range(8):
+        sums = [
+            s + tiles[k, i // 4, i % 4, :, a].astype(F32).reshape(16, 8, width).sum(axis=0)
             for a, s in enumerate(sums)
-        )
-
-    zero = jnp.zeros((8, width), F32)
-    sums = lax.fori_loop(0, 8, add_up, (zero, zero), unroll=True)
+        ]
     means = [s.sum(axis=0, keepdims=True) / total for s in sums]
-
-    def centre(i, _):
-        core, z = i // 4, i % 4
-        offset = tiles[k, core, z, :, 0].astype(F32).reshape(128, width) - means[0]
-        grad = tiles[k, core, z, :, 1].astype(F32).reshape(128, width) - means[1]
-        rows = pl.ds(pl.multiple_of(i * 128, 128), 128)
+    for i in range(8):
+        offset = tiles[k, i // 4, i % 4, :, 0].astype(F32).reshape(128, width) - means[0]
+        grad = tiles[k, i // 4, i % 4, :, 1].astype(F32).reshape(128, width) - means[1]
+        rows = slice(i * 128, (i + 1) * 128)
         mixed[rows, 0:width] = offset.astype(BF16)
-        mixed[rows, width : 2 * width] = (weight[rows, :] * offset + grad).astype(BF16)
-        return 0
-
-    lax.fori_loop(0, 8, centre, 0)
-
-    def part(i, _):
-        rows = pl.ds(pl.multiple_of(i * 256, 256), 256)
+        mixed[rows, width:] = (weight[rows, :] * offset + grad).astype(BF16)
+    for i in range(total // BLOCK):
+        rows = slice(i * BLOCK, (i + 1) * BLOCK)
         store(rows, jnp.dot(row_t[rows, :], mixed[...], preferred_element_type=F32) / total)
-        return 0
-
-    lax.fori_loop(0, 4, part, 0)
 
 
 def exchange(
     derivs, grads, energies, tiles, row_t, weight, done,
-    energy, xb, yb, r0, ra, rb, ez, ex, ey, mixed,
-    s_x, s_y, s_z, s_c, s_r, s_e, x_sem, y_sem, z_sem, c_sem, r_sem, e_sem,
+    energy, zb, fb, xb, yb, r0, ra, rb, ez, ex, ey, mixed,
+    s_f, s_x, s_y, s_z, s_c, s_r, s_e, fz_sem, fx_sem, slab_sem, x_sem, y_sem, z_sem, c_sem, r_sem, e_sem,
 ):
     x, y, z, core = place()
     chunks = tiles.shape[0]
@@ -95,7 +90,7 @@
 
     own = lax.broadcasted_iota(jnp.int32, (8, 8), 0) == lax.broadcasted_iota(jnp.int32, (8, 8), 1)
     column = jnp.where(own, energies[...], 0).sum(axis=1, keepdims=True)
-    energy[...] = jnp.broadcast_to(column, (8, LANES))
+    energy[0] = jnp.broadcast_to(column, (8, LANES))
 
     barrier = pltpu.get_barrier_semaphore()
     for peer in mates + others + along_x + along_y:
@@ -125,6 +120,29 @@
             send(yb.at[k, peer[2] % 2], tiles.at[k, core, z], s_z, z_sem.at[k], peer)
         keep(yb.at[k, z % 2], tiles.at[k, core, z], z_sem.at[k])
 
+    @jax.named_scope("first_z")
+    def first_z(k):
+        for a, source in enumerate((derivs, grads)):
+            for peer in mates:
+                block = source.at[peer[2] % 2, :, :, k // quarter, k % quarter]
+                send(block, zb.at[k, :, :, z, a], s_f.at[0], fz_sem.at[k], peer)
+            block = source.at[z % 2, :, :, k // quarter, k % quarter]
+            keep(block, zb.at[k, :, :, z, a], fz_sem.at[k])
+
+    @jax.named_scope("first_x")
+    def first_x(k):
+        await_bytes(zb.at[k], fz_sem.at[k])
+        for peer in along_x:
+            send(zb.at[k, peer[0]], fb.at[k, :, :, :, x], s_f.at[1], fx_sem.at[k], peer)
+        keep(zb.at[k, x], fb.at[k, :, :, :, x], fx_sem.at[k])
+
+    @jax.named_scope("first_y")
+    def first_y(k):
+        await_bytes(fb.at[k], fx_sem.at[k])
+        for peer in along_y:
+            send(fb.at[k, peer[1]], tiles.at[k, core, :, y], s_f.at[2], z_sem.at[k], peer)
+        keep(fb.at[k, y], tiles.at[k, core, :, y], z_sem.at[k])
+
     @jax.named_scope("to_partner")
     def to_partner(k):
         await_bytes(tiles.at[k, core], z_sem.at[k])
@@ -142,29 +160,67 @@
     def when(condition, stage, k):
         pl.when(condition)(functools.partial(stage, k))
 
+    @jax.named_scope("slab_direct")
+    def slab_direct(piece):
+        part = (slice(None), piece // 4, piece % 4)
+        for peer in along_y[1:]:
+            block = ra.at[(y, *part)]
+            send(block, block, s_r.at[4], slab_sem.at[0, piece], peer)
+        for peer in along_x[1:]:
+            block = rb.at[(x, *part)]
+            send(block, block, s_r.at[5], slab_sem.at[1, piece], peer)
+
+    @jax.named_scope("slab_relay")
+    def slab_relay(piece):
+        part = (slice(None), piece // 4, piece % 4)
+        back, ahead = 3 - 2 * (piece % 2), 1 + 2 * (piece % 2)
+        await_bytes(ra.at[0:2, :, 0, 0], slab_sem.at[0, piece])
+        block = ra.at[((y + back) % 4, *part)]
+        send(block, block, s_r.at[6], r_sem.at[3], (x, (y + ahead) % 4, z, core))
+        await_bytes(rb.at[0:2, :, 0, 0], slab_sem.at[1, piece])
+        block = rb.at[((x + back) % 4, *part)]
+        send(block, block, s_r.at[7], r_sem.at[4], ((x + ahead) % 4, y, z, core))
+
+    rest = chunks - EARLY_Z
+
     def finished(i):
-        return jnp.clip(jnp.minimum(2 * (i + 1 - FIRST), i - LAG_Y - LAG_Z), 0, early)
+        return jnp.clip(jnp.minimum(PACE * (i + 1 - FIRST), i - LAG_Y - LAG_Z + EARLY_Z), 0, early)
 
     def step(i):
-        when(i + AHEAD < chunks, to_x, i + AHEAD)
-        when(i < chunks, to_y, i)
-        when((i >= LAG_Y) & (i < chunks + LAG_Y), to_z, i - LAG_Y)
+        when(i < rest, to_y, i + EARLY_Z)
+        when(i + AHEAD < rest, to_x, i + AHEAD + EARLY_Z)
+        when((i >= LAG_Y + 2) & (i < rest + LAG_Y), to_z, i - LAG_Y + EARLY_Z)
         late = i - LAG_Y - LAG_Z
-        when((late >= 0) & (late < chunks), to_partner, late)
-
-    to_x(0)
+        when((late >= 0) & (late < rest), to_partner, late + EARLY_Z)
+        for j in range(PIECES):
+            piece = (i - SLAB_STEP) * PIECES + j
+            when((piece >= 0) & (piece < 8), slab_direct, piece)
+            piece = piece - RELAY_LAG * PIECES
+            when((piece >= 0) & (piece < 8), slab_relay, piece)
+        first = i - F_STEP
+        when((first >= 0) & (first < EARLY_Z), first_x, first)
+        when((first >= F_LAG) & (first < EARLY_Z + F_LAG), first_y, first - F_LAG)
+        when((first >= 2 * F_LAG) & (first < EARLY_Z + 2 * F_LAG), to_partner, first - 2 * F_LAG)
+
+    lane = lax.broadcasted_iota(jnp.int32, (8, LANES), 1)
+
+    def gather(blocks, stride):
+        return sum(jnp.where((lane // stride) % 4 == i, blocks[i], 0) for i in range(4))
+
+    to_x(EARLY_Z)
     for group, sem in ((mates, 0), (others, 1)):
         for peer in group:
             block = derivs.at[0, 0, peer[2] // 2, pl.ds(peer[3] * 2, 2)]
             send(block, r0.at[core, z], s_r.at[sem], r_sem.at[0], peer)
     keep(derivs.at[0, 0, z // 2, pl.ds(core * 2, 2)], r0.at[core, z], r_sem.at[0])
     for peer in mates:
-        send(energy, ez.at[z], s_e.at[0], e_sem.at[0], peer)
-    keep(energy, ez.at[z], e_sem.at[0])
-    for k in range(1, AHEAD):
-        to_x(k)
-
-    step(0)
+        send(energy.at[0], ez.at[z], s_e.at[0], e_sem.at[0], peer)
+    keep(energy.at[0], ez.at[z], e_sem.at[0])
+    for k in range(EARLY_Z):
+        first_z(k)
+    pl.loop(EARLY_Z + 1, EARLY_Z + AT_ONCE)(to_x)
+    to_y(EARLY_Z)
+
     with jax.named_scope("r1"):
         await_bytes(r0, r_sem.at[0])
         for peer in along_x:
@@ -173,38 +229,41 @@
         for peer in along_y:
             send(r0.at[:, :, 1], rb.at[x, y], s_r.at[3], r_sem.at[2], peer)
         keep(r0.at[:, :, 1], rb.at[x, y], r_sem.at[2])
-        await_bytes(ez, e_sem.at[0])
+    pl.loop(EARLY_Z + AT_ONCE, EARLY_Z + AHEAD + 1)(to_x)
+    to_y(EARLY_Z + 1)
+    to_x(EARLY_Z + AHEAD + 1)
+    await_bytes(ez, e_sem.at[0])
+    energy[1] = gather(ez, 32)
+    to_z(EARLY_Z)
+    to_y(EARLY_Z + 2)
+    to_x(EARLY_Z + AHEAD + 2)
+    to_z(EARLY_Z + 1)
+    pl.loop(3, SLAB_STEP)(step)
+    with jax.named_scope("r2"):
         for peer in along_x:
-            send(ez, ex.at[x], s_e.at[1], e_sem.at[1], peer)
-        keep(ez, ex.at[x], e_sem.at[1])
-    pl.loop(1, SLAB_STEP)(step)
-    with jax.named_scope("r2"):
+            send(energy.at[1], ex.at[x], s_e.at[1], e_sem.at[1], peer)
+        keep(energy.at[1], ex.at[x], e_sem.at[1])
         await_bytes(ra.at[y], r_sem.at[1])
         await_bytes(rb.at[x], r_sem.at[2])
-        await_bytes(ex, e_sem.at[1])
-
-    @pl.loop(SLAB_STEP, SLAB_STEP + 4)
-    def _(i):
-        step(i)
-        for side in range(2):
-            part = (side, i - SLAB_STEP)
-            for peer in along_y:
-                send(ra.at[(y, slice(None), *part)], ra.at[(y, slice(None), *part)], s_r.at[4], r_sem.at[3], peer)
-            for peer in along_x:
-                send(rb.at[(x, slice(None), *part)], rb.at[(x, slice(None), *part)], s_r.at[5], r_sem.at[4], peer)
-
+
+    middle = SLAB_STEP + 3
+    pl.loop(SLAB_STEP, middle)(step)
+    await_bytes(ex, e_sem.at[1])
+    energy[2] = gather(ex, 8)
+    step(middle)
     for peer in along_y:
-        send(ex, ey.at[core, y], s_e.at[2], e_sem.at[2], peer)
-    keep(ex, ey.at[core, y], e_sem.at[2])
-    pl.loop(SLAB_STEP + 4, FIRST - 1)(step)
+        send(energy.at[2], ey.at[y], s_e.at[2], e_sem.at[2], peer)
+    keep(energy.at[2], ey.at[y], e_sem.at[2])
+    pl.loop(middle + 1, FIRST - 1)(step)
     with jax.named_scope("e"):
-        await_bytes(ey.at[core], e_sem.at[2])
-    send(ey.at[core], ey.at[core], s_e.at[3], e_sem.at[3], partner)
+        await_bytes(ey, e_sem.at[2])
+        energy[3] = gather(ey, 2)
     step(FIRST - 1)
+    send(energy.at[3], energy.at[4], s_e.at[3], e_sem.at[3], partner)
 
     with jax.named_scope("r3"):
-        await_bytes(ra.at[0:3], r_sem.at[3])
-        await_bytes(rb.at[0:3], r_sem.at[4])
+        await_bytes(ra.at[0], r_sem.at[3])
+        await_bytes(rb.at[0], r_sem.at[4])
 
     @pl.loop(0, quarter)
     @jax.named_scope("prep")
@@ -222,13 +281,15 @@
             for i, block in enumerate(blocks):
                 row_t[rows, i * 128 : (i + 1) * 128] = (block - mean).T.astype(BF16)
 
-    await_bytes(ey.at[1 - core], e_sem.at[3])
-    mean_energy = ey[...].reshape(128, 8, LANES).sum(axis=0).sum(axis=0, keepdims=True) / 1024
-    for i in range(8):
-        every = ey[i // 4, :, :, i % 4].reshape(128, LANES)
-        weight[i * 128 : (i + 1) * 128, :] = every - mean_energy
-
-    @pl.loop(FIRST, chunks + LAG_Y + LAG_Z)
+    with jax.named_scope("w"):
+        await_bytes(energy.at[4], e_sem.at[3])
+        every = jnp.where(lane % 2 == core, energy[3], energy[4])
+        every = every - every.sum(axis=0, keepdims=True).sum(axis=1, keepdims=True) / 1024
+        for i in range(128):
+            at = (i // 16 % 4) * 32 + (i % 4) * 8 + (i // 4 % 4) * 2 + i // 64
+            weight[i * 8 : i * 8 + 8, :] = jnp.broadcast_to(every[:, at : at + 1], (8, LANES))
+
+    @pl.loop(FIRST, rest + LAG_Y + LAG_Z)
     def _(i):
         step(i)
         pl.loop(finished(i - 1), finished(i))(finish)
@@ -236,20 +297,25 @@
     pl.loop(finished(chunks + LAG_Y + LAG_Z - 1), early)(finish)
     pl.loop(early, chunks)(lambda k: await_bytes(tiles.at[k, 1 - core], c_sem.at[k]))
 
-    await_bytes(xb.at[:, :, 0:3], s_x)
-    await_bytes(yb.at[:, :, 0:3], s_y)
-    await_bytes(tiles.at[:, 0, 0:3], s_z)
+    await_bytes(zb.at[:, 0:3], s_f.at[0])
+    await_bytes(fb.at[:, 0:3], s_f.at[1])
+    await_bytes(fb.at[:, 0:3], s_f.at[2])
+    await_bytes(xb.at[EARLY_Z:, :, 0:3], s_x)
+    await_bytes(yb.at[EARLY_Z:, :, 0:3], s_y)
+    await_bytes(tiles.at[EARLY_Z:, 0, 0:3], s_z)
     await_bytes(tiles.at[:, 0], s_c)
     await_bytes(r0.at[0, 0:3], s_r.at[0])
     await_bytes(r0.at[0], s_r.at[1])
     await_bytes(ra.at[0, 0:3], s_r.at[2])
     await_bytes(rb.at[0, 0:3], s_r.at[3])
-    await_bytes(ra.at[0:3], s_r.at[4])
-    await_bytes(rb.at[0:3], s_r.at[5])
+    await_bytes(ra.at[0:2], s_r.at[4])
+    await_bytes(rb.at[0:2], s_r.at[5])
+    await_bytes(ra.at[0], s_r.at[6])
+    await_bytes(rb.at[0], s_r.at[7])
     await_bytes(ez.at[0:3], s_e.at[0])
     await_bytes(ex.at[0:3], s_e.at[1])
-    await_bytes(ey.at[0, 0:3], s_e.at[2])
-    await_bytes(ey.at[0], s_e.at[3])
+    await_bytes(ey.at[0:3], s_e.at[2])
+    await_bytes(energy.at[3], s_e.at[3])
 
 
 def write(tiles, row_t, weight, done, corr, hamil, late, mixed, sem):
@@ -298,17 +364,19 @@
         in_specs=[hbm, hbm, vmem],
         out_specs=(vmem,) * 4,
         scratch_shapes=[
-            pltpu.VMEM((8, LANES), F32),
+            pltpu.VMEM((5, 8, LANES), F32),
+            pltpu.VMEM((EARLY_Z, 4, 4, 4, 2, 8, WIDTH), BF16),
+            pltpu.VMEM((EARLY_Z, 4, 4, 2, 4, 8, WIDTH), BF16),
             pltpu.VMEM((chunks, 2, 4, 2, 4, 8, WIDTH), BF16),
             pltpu.VMEM((chunks, 2, 4, 2, 4, 8, WIDTH), BF16),
             pltpu.VMEM((2, 4, 2, quarter, 8, WIDTH), BF16),
             pltpu.VMEM((4, 4, 2, 4, quarter, 8, WIDTH), BF16),
             pltpu.VMEM((4, 4, 2, 4, quarter, 8, WIDTH), BF16),
             pltpu.VMEM((4, 8, LANES), F32),
-            pltpu.VMEM((4, 4, 8, LANES), F32),
-            pltpu.VMEM((2, 4, 4, 4, 8, LANES), F32),
+            pltpu.VMEM((4, 8, LANES), F32),
+            pltpu.VMEM((4, 8, LANES), F32),
             pltpu.VMEM((1024, 2 * WIDTH), BF16),
-            dma, dma, dma, dma, dma((6,)), dma((4,)),
+            dma((3,)), dma, dma, dma, dma, dma((8,)), dma((4,)), dma((EARLY_Z,)), dma((EARLY_Z,)), dma((2, 8)),
             dma((chunks,)), dma((chunks,)), dma((chunks,)), dma((chunks,)), dma((5,)), dma((4,)),
         ],
         compiler_params=pltpu.CompilerParams(

time: 80.3 us -> 74.1 us (0.923)
  Pallas kernels: 78.9 us -> 72.6 us
    pallas_call x1, Pallas kernels: 73.1 us -> 66.8 us  [body(): pl.pallas_call(exchange, out_shape=(pltpu.VMEM((chunks, 2, 4, 4, 2, 4, 8,...]
where the time goes in v3:
time: 74.1 us; the launch traced here: 73.9 us
  Pallas kernels  72.6 us (98%)
    pallas_call x1, Pallas kernels, body(): pl.pallas_call(exchange, out_shape=(pltpu.VMEM((chunks, 2, 4, 4, 2, 4, 8,...  66.8 us
    pallas_call x1, Pallas kernels, body(): pl.pallas_call(write, out_shape=(out, out), in_specs=[vmem] * 4, out_spec...  5.81 us

profile of v3, /device:TPU:1, one launch (start us, length us, event | category | flops | bytes accessed | tf_op | source)
XLA Modules:
  0.0 73.9 jit_solution(16117622498696950362)
XLA Ops:
  0.6 0.0 copy-start
  0.6 0.6 copy-done
  1.3 66.8 %exchange.1 = (bf16[16,2,4,4,2,4,8,128]{7,6,5,4,3,2,1,0:T(8,128)(2,1)S(1)}, bf16[1024,1024]{1,0:T(8,128)(2,1)S(1)}, f32[1024,128]{1,0:T(8,128)S(1)}, f32[12,1024,256]{2,1,0:T(8,128)S(1)}) custom-call(bf16[2,4,4,4,4,8,128]{6,5,4,3,2,1,0:T(8,128)(2,1)} %bitcast.8, bf16[2,4,4,4,4,8,128]{6,5,4,3,2,1,0:T(8,128)(2,1)} %bitcast.9, f32[1,8]{1,0:T(1,128)S(1)} %bitcast.7), custom_call_target="tpu_custom_call" | custom-call | tf_op jit(solution)/shard_map/exchange/pallas_call | solution.py:356
  68.1 5.8 %write.1 = (f32[1024,2048]{1,0:T(8,128)}, f32[1024,2048]{1,0:T(8,128)}) custom-call(bf16[16,2,4,4,2,4,8,128]{7,6,5,4,3,2,1,0:T(8,128)(2,1)S(1)} %get-tuple-element.6.tiles, bf16[1024,1024]{1,0:T(8,128)(2,1)S(1)} %get-tuple-element.7.row_t, f32[1024,128]{1,0:T(8,128)S(1)} %get-tuple-element.8.weight, f32[12,1024,256]{2,1,0:T(8,128)S(1)} %get-tuple-element.9.done), custom_call_target="tpu_custom_call" | custom-call | tf_op jit(solution)/shard_map/write/pallas_call | solution.py:388
Async XLA Ops:
  0.6 0.7 copy-start

commit v4 on v3

--- a/solution.py
+++ b/solution.py
@@ -10,17 +10,16 @@
 MESH = pl.DeviceIdType.MESH
 LANES = 128
 WIDTH = 128
-EARLY_Z = 1
-F_STEP = 3
-F_LAG = 2
+EARLY_Z = 2
+F_STEP = 6
+F_LAG = 3
 AT_ONCE = 2
 AHEAD = 3
 LAG_Y = 2
 LAG_Z = 3
-SLAB_STEP = 3
-FIRST = 13
-PIECES = 1
-RELAY_LAG = 2
+SLAB_FIRST = 2
+FIRST = 12
+RELAY_LAG = 3
 PACE = 3
 BLOCK = 256
 TAIL = 4
@@ -149,7 +148,9 @@
         send(tiles.at[k, core], tiles.at[k, core], s_c, c_sem.at[k], partner)
 
     @jax.named_scope("finish")
-    def finish(k):
+    def finish(j):
+        turn = early - EARLY_Z
+        k = jnp.where(j < turn, j + EARLY_Z, j - turn)
         await_bytes(tiles.at[k, 1 - core], c_sem.at[k])
 
         def store(rows, value):
@@ -184,7 +185,7 @@
     rest = chunks - EARLY_Z
 
     def finished(i):
-        return jnp.clip(jnp.minimum(PACE * (i + 1 - FIRST), i - LAG_Y - LAG_Z + EARLY_Z), 0, early)
+        return jnp.clip(jnp.minimum(PACE * (i + 1 - FIRST), i - LAG_Y - LAG_Z), 0, early)
 
     def step(i):
         when(i < rest, to_y, i + EARLY_Z)
@@ -192,11 +193,10 @@
         when((i >= LAG_Y + 2) & (i < rest + LAG_Y), to_z, i - LAG_Y + EARLY_Z)
         late = i - LAG_Y - LAG_Z
         when((late >= 0) & (late < rest), to_partner, late + EARLY_Z)
-        for j in range(PIECES):
-            piece = (i - SLAB_STEP) * PIECES + j
-            when((piece >= 0) & (piece < 8), slab_direct, piece)
-            piece = piece - RELAY_LAG * PIECES
-            when((piece >= 0) & (piece < 8), slab_relay, piece)
+        piece = i - 2 + SLAB_FIRST
+        when(piece < 8, slab_direct, piece)
+        piece = piece - RELAY_LAG
+        when((piece >= 0) & (piece < 8), slab_relay, piece)
         first = i - F_STEP
         when((first >= 0) & (first < EARLY_Z), first_x, first)
         when((first >= F_LAG) & (first < EARLY_Z + F_LAG), first_y, first - F_LAG)
@@ -235,19 +235,20 @@
     await_bytes(ez, e_sem.at[0])
     energy[1] = gather(ez, 32)
     to_z(EARLY_Z)
+    with jax.named_scope("r2"):
+        await_bytes(ra.at[y], r_sem.at[1])
+        await_bytes(rb.at[x], r_sem.at[2])
+        for piece in range(SLAB_FIRST):
+            slab_direct(piece)
     to_y(EARLY_Z + 2)
     to_x(EARLY_Z + AHEAD + 2)
     to_z(EARLY_Z + 1)
-    pl.loop(3, SLAB_STEP)(step)
-    with jax.named_scope("r2"):
-        for peer in along_x:
-            send(energy.at[1], ex.at[x], s_e.at[1], e_sem.at[1], peer)
-        keep(energy.at[1], ex.at[x], e_sem.at[1])
-        await_bytes(ra.at[y], r_sem.at[1])
-        await_bytes(rb.at[x], r_sem.at[2])
-
-    middle = SLAB_STEP + 3
-    pl.loop(SLAB_STEP, middle)(step)
+    slab_direct(SLAB_FIRST)
+    for peer in along_x:
+        send(energy.at[1], ex.at[x], s_e.at[1], e_sem.at[1], peer)
+    keep(energy.at[1], ex.at[x], e_sem.at[1])
+    middle = 6
+    pl.loop(3, middle)(step)
     await_bytes(ex, e_sem.at[1])
     energy[2] = gather(ex, 8)
     step(middle)

time: 74.1 us -> 71.9 us (0.970)
  Pallas kernels: 72.6 us -> 70.5 us
    pallas_call x1, Pallas kernels: 66.8 us -> 64.7 us  [body(): pl.pallas_call(exchange, out_shape=(pltpu.VMEM((chunks, 2, 4, 4, 2, 4, 8,...]
where the time goes in v4:
time: 71.9 us; the launch traced here: 71.8 us
  Pallas kernels  70.5 us (98%)
    pallas_call x1, Pallas kernels, body(): pl.pallas_call(exchange, out_shape=(pltpu.VMEM((chunks, 2, 4, 4, 2, 4, 8,...  64.7 us
    pallas_call x1, Pallas kernels, body(): pl.pallas_call(write, out_shape=(out, out), in_specs=[vmem] * 4, out_spec...  5.81 us

profile of v4, /device:TPU:1, one launch (start us, length us, event | category | flops | bytes accessed | tf_op | source)
XLA Modules:
  0.0 71.8 jit_solution(17808527922379747553)
XLA Ops:
  0.6 0.0 copy-start
  0.6 0.6 copy-done
  1.3 64.7 %exchange.1 = (bf16[16,2,4,4,2,4,8,128]{7,6,5,4,3,2,1,0:T(8,128)(2,1)S(1)}, bf16[1024,1024]{1,0:T(8,128)(2,1)S(1)}, f32[1024,128]{1,0:T(8,128)S(1)}, f32[12,1024,256]{2,1,0:T(8,128)S(1)}) custom-call(bf16[2,4,4,4,4,8,128]{6,5,4,3,2,1,0:T(8,128)(2,1)} %bitcast.8, bf16[2,4,4,4,4,8,128]{6,5,4,3,2,1,0:T(8,128)(2,1)} %bitcast.9, f32[1,8]{1,0:T(1,128)S(1)} %bitcast.7), custom_call_target="tpu_custom_call" | custom-call | tf_op jit(solution)/shard_map/exchange/pallas_call | solution.py:357
  66.0 5.8 %write.1 = (f32[1024,2048]{1,0:T(8,128)}, f32[1024,2048]{1,0:T(8,128)}) custom-call(bf16[16,2,4,4,2,4,8,128]{7,6,5,4,3,2,1,0:T(8,128)(2,1)S(1)} %get-tuple-element.6.tiles, bf16[1024,1024]{1,0:T(8,128)(2,1)S(1)} %get-tuple-element.7.row_t, f32[1024,128]{1,0:T(8,128)S(1)} %get-tuple-element.8.weight, f32[12,1024,256]{2,1,0:T(8,128)S(1)} %get-tuple-element.9.done), custom_call_target="tpu_custom_call" | custom-call | tf_op jit(solution)/shard_map/write/pallas_call | solution.py:389
Async XLA Ops:
  0.6 0.7 copy-start

commit v5 on v4

--- a/solution.py
+++ b/solution.py
@@ -16,7 +16,7 @@
 AT_ONCE = 2
 AHEAD = 3
 LAG_Y = 2
-LAG_Z = 3
+LAG_Z = 4
 SLAB_FIRST = 2
 FIRST = 12
 RELAY_LAG = 3
@@ -207,19 +207,16 @@
     def gather(blocks, stride):
         return sum(jnp.where((lane // stride) % 4 == i, blocks[i], 0) for i in range(4))
 
-    to_x(EARLY_Z)
     for group, sem in ((mates, 0), (others, 1)):
         for peer in group:
             block = derivs.at[0, 0, peer[2] // 2, pl.ds(peer[3] * 2, 2)]
             send(block, r0.at[core, z], s_r.at[sem], r_sem.at[0], peer)
     keep(derivs.at[0, 0, z // 2, pl.ds(core * 2, 2)], r0.at[core, z], r_sem.at[0])
+    to_x(EARLY_Z)
     for peer in mates:
         send(energy.at[0], ez.at[z], s_e.at[0], e_sem.at[0], peer)
     keep(energy.at[0], ez.at[z], e_sem.at[0])
-    for k in range(EARLY_Z):
-        first_z(k)
     pl.loop(EARLY_Z + 1, EARLY_Z + AT_ONCE)(to_x)
-    to_y(EARLY_Z)
 
     with jax.named_scope("r1"):
         await_bytes(r0, r_sem.at[0])
@@ -229,6 +226,9 @@
         for peer in along_y:
             send(r0.at[:, :, 1], rb.at[x, y], s_r.at[3], r_sem.at[2], peer)
         keep(r0.at[:, :, 1], rb.at[x, y], r_sem.at[2])
+    for k in range(EARLY_Z):
+        first_z(k)
+    to_y(EARLY_Z)
     pl.loop(EARLY_Z + AT_ONCE, EARLY_Z + AHEAD + 1)(to_x)
     to_y(EARLY_Z + 1)
     to_x(EARLY_Z + AHEAD + 1)

time: 71.9 us -> 72.1 us (level)
  no operation moved by 1% of the time
where the time goes in v5:
time: 72.1 us; the launch traced here: 71.9 us
  Pallas kernels  70.6 us (98%)
    pallas_call x1, Pallas kernels, body(): pl.pallas_call(exchange, out_shape=(pltpu.VMEM((chunks, 2, 4, 4, 2, 4, 8,...  64.8 us
    pallas_call x1, Pallas kernels, body(): pl.pallas_call(write, out_shape=(out, out), in_specs=[vmem] * 4, out_spec...  5.81 us

profile of v5, /device:TPU:1, one launch (start us, length us, event | category | flops | bytes accessed | tf_op | source)
XLA Modules:
  0.0 71.9 jit_solution(8701593802498664838)
XLA Ops:
  0.6 0.0 copy-start
  0.6 0.6 copy-done
  1.3 64.8 %exchange.1 = (bf16[16,2,4,4,2,4,8,128]{7,6,5,4,3,2,1,0:T(8,128)(2,1)S(1)}, bf16[1024,1024]{1,0:T(8,128)(2,1)S(1)}, f32[1024,128]{1,0:T(8,128)S(1)}, f32[12,1024,256]{2,1,0:T(8,128)S(1)}) custom-call(bf16[2,4,4,4,4,8,128]{6,5,4,3,2,1,0:T(8,128)(2,1)} %bitcast.8, bf16[2,4,4,4,4,8,128]{6,5,4,3,2,1,0:T(8,128)(2,1)} %bitcast.9, f32[1,8]{1,0:T(1,128)S(1)} %bitcast.7), custom_call_target="tpu_custom_call" | custom-call | tf_op jit(solution)/shard_map/exchange/pallas_call | solution.py:357
  66.1 5.8 %write.1 = (f32[1024,2048]{1,0:T(8,128)}, f32[1024,2048]{1,0:T(8,128)}) custom-call(bf16[16,2,4,4,2,4,8,128]{7,6,5,4,3,2,1,0:T(8,128)(2,1)S(1)} %get-tuple-element.6.tiles, bf16[1024,1024]{1,0:T(8,128)(2,1)S(1)} %get-tuple-element.7.row_t, f32[1024,128]{1,0:T(8,128)S(1)} %get-tuple-element.8.weight, f32[12,1024,256]{2,1,0:T(8,128)S(1)} %get-tuple-element.9.done), custom_call_target="tpu_custom_call" | custom-call | tf_op jit(solution)/shard_map/write/pallas_call | solution.py:389
Async XLA Ops:
  0.6 0.7 copy-start
